TPU v7x, 768 devices: a whole 4x8x12 slice. The times are simulated.
768 devices in a mesh: gx: 12 (over z), gy: 64 (over y, x, core).
Axes of the slice: x: 4, y: 8, z: 12, core: 2. Of those that a mesh axis runs over, the one named last changes fastest.
Arguments:
- ensemble: float32 [288, 4096, 128], P('gx', 'gy'), may hold values from -30 to 30
- coefficients: float32 [3, 288, 4096], P(None, 'gx', 'gy'), may hold values from -0.3 to 0.3
- obs_owner: int32 [1024], replicated, may hold values from 0 to 767, as said below
- obs_cell: int32 [1024], replicated, may hold values from 0 to 1535
- obs_batch: int32 [1024], replicated, may hold values from 0 to 1, as said below
- obs_value: float32 [1024], replicated, may hold values from -6 to 6
- obs_var: float32 [1024], replicated, may hold values from 0.5 to 5
Outputs:
- analysis: float32 [288, 4096, 128], P('gx', 'gy')
Inputs may be any that keep to these rules, and one draw needn't show every extreme that they name: Exactly 512 observations have obs_batch 0 and 512 have 1; in each batch no tile owns more than 2 observations and some tile owns exactly 2. `obs_owner`: owner tiles are numbered by the first tile index times 64 plus the second.
All inputs are finite; a program needn't handle non-finite values.
Results may differ from a plain program's by a relative error of at most 0.00014.
Values sent between devices are 32-bit elements; how exact they have to be, the bound alone decides.
No kernel may reach another device: no remote copies, remote signals or barrier semaphores. Data moves between devices by JAX's collectives and lax.ppermute only.
A program may use at most 32 MiB of HBM per device.

v0:
```python
import functools

import jax
import jax.numpy as jnp
from jax import lax
from jax.experimental import pallas as pl
from jax.experimental.pallas import tpu as pltpu
from jax.sharding import PartitionSpec as P

STEPS = 4
CAP = 2
GROUP = 12
BATCHES = 2
EPS = 1e-05
GY_FACTORS = {64: (8, 4, 2), 8: (2, 2, 2)}


def neighbours(axis):
    size = lax.axis_size(axis)
    up = [(i, i + 1) for i in range(size - 1)]
    return up, [(j, i) for i, j in up]


def exchange(to_next, to_previous, axis):
    up, down = neighbours(axis)
    return lax.ppermute(to_next, axis, up), lax.ppermute(to_previous, axis, down)


def in_vmem():
    return pl.BlockSpec(memory_space=pltpu.VMEM)


def in_smem():
    return pl.BlockSpec(memory_space=pltpu.SMEM)


def grant(mib):
    return pltpu.CompilerParams(vmem_limit_bytes=mib << 20)


LINES = 8
MARGIN = 8


def pack_x_kernel(field_ref, whole_ref, first_ref, last_ref, coefs_ref, sems):
    tile_x, tile_y, _ = field_ref.shape
    kinds = coefs_ref.shape[0]
    copies = [pltpu.make_async_copy(whole_ref, coefs_ref, sems.at[2])]
    for index, (out_ref, start) in enumerate(((first_ref, 0), (last_ref, tile_x - STEPS))):
        copies.append(
            pltpu.make_async_copy(
                field_ref.at[pl.ds(start, STEPS)], out_ref.at[:, pl.ds(0, tile_y)], sems.at[index]
            )
        )
    for copy in copies:
        copy.start()
    for out_ref in (first_ref, last_ref):
        out_ref[:, tile_y:, :] = jnp.zeros_like(out_ref[:, tile_y:, :])
    copies[0].wait()
    for out_ref, start in ((first_ref, 0), (last_ref, tile_x - STEPS)):
        for kind in range(kinds):
            part = coefs_ref[kind, start : start + STEPS, :]
            for i in range(STEPS):
                out_ref[i, tile_y + kind : tile_y + kind + 1, :tile_y] = part[i : i + 1, :]
    for copy in copies[1:]:
        copy.wait()


def pack_x(field, coefs):
    _, tile_y, members = field.shape
    slab = jax.ShapeDtypeStruct((STEPS, tile_y + LINES, members), jnp.float32)
    return pl.pallas_call(
        pack_x_kernel,
        name="pack_x",
        out_shape=(slab, slab, jax.ShapeDtypeStruct(coefs.shape, jnp.float32)),
        in_specs=[pl.BlockSpec(memory_space=pl.ANY)] * 2,
        out_specs=(in_vmem(),) * 3,
        scratch_shapes=[pltpu.SemaphoreType.DMA((3,))],
        compiler_params=grant(4),
    )(*(pltpu.with_memory_space_constraint(a, pltpu.HBM) for a in (field, coefs)))


def pack_y_kernel(field_ref, coefs_ref, before_ref, after_ref, first_ref, last_ref):
    tile_x, tile_y, _ = field_ref.shape
    kinds = coefs_ref.shape[0]
    inner = slice(STEPS, STEPS + tile_x)
    outer = slice(STEPS + tile_x, 2 * STEPS + tile_x)
    for out_ref, start in ((first_ref, 0), (last_ref, tile_y - STEPS)):
        edge = slice(start, start + STEPS)
        out_ref[:STEPS, :STEPS, :] = before_ref[:, edge, :]
        out_ref[inner, :STEPS, :] = field_ref[:, edge, :]
        out_ref[outer, :STEPS, :] = after_ref[:, edge, :]
        out_ref[inner, STEPS:, :] = jnp.zeros_like(out_ref[inner, STEPS:, :])
        out_ref[:STEPS, STEPS:, :] = before_ref[:, tile_y : tile_y + LINES - STEPS, :]
        out_ref[outer, STEPS:, :] = after_ref[:, tile_y : tile_y + LINES - STEPS, :]
    for kind in range(kinds):
        part = coefs_ref[kind]
        for i in range(tile_x):
            for out_ref in (first_ref, last_ref):
                out_ref[STEPS + i, STEPS + kind : STEPS + kind + 1, :tile_y] = part[i : i + 1, :]


def pack_y(field, coefs, before, after):
    tile_x, _, members = field.shape
    slab = jax.ShapeDtypeStruct((tile_x + 2 * STEPS, LINES, members), jnp.float32)
    return pl.pallas_call(
        pack_y_kernel,
        name="pack_y",
        out_shape=(slab, slab),
        in_specs=[in_vmem()] * 4,
        out_specs=(in_vmem(), in_vmem()),
        compiler_params=grant(8),
    )(field, coefs, before, after)


def advance(west, centre, east, diffuse, speed_x, speed_y):
    size = centre.shape[0]
    north = pltpu.roll(centre, size - 1, 0)
    south = pltpu.roll(centre, 1, 0)
    spread = east + west + north + south - 4.0 * centre
    carried = 0.5 * (speed_x * (east - west) + speed_y * (north - south))
    return centre + diffuse * spread - (1.0 + 0.5 * jnp.tanh(centre)) * carried


def look_kernel(
    copies,
    cells_ref,
    field_ref,
    coefs_ref,
    before_ref,
    after_ref,
    left_ref,
    right_ref,
    padded_ref,
    columns_ref,
    priors_ref,
    lines_ref,
    last_ref,
):
    tile_x, tile_y, members = field_ref.shape
    kinds = coefs_ref.shape[0]
    high_x, high_y = padded_ref.shape[0], padded_ref.shape[1]
    inner = slice(STEPS, STEPS + tile_x)
    outer = slice(STEPS + tile_x, high_x)
    own = slice(MARGIN, MARGIN + tile_y)
    padded_ref[:, :MARGIN, :] = jnp.zeros((high_x, MARGIN, members), jnp.float32)
    padded_ref[:, MARGIN + tile_y :, :] = jnp.zeros(
        (high_x, high_y - MARGIN - tile_y, members), jnp.float32
    )
    padded_ref[:STEPS, own, :] = before_ref[:, :tile_y, :]
    padded_ref[inner, own, :] = field_ref[...]
    padded_ref[outer, own, :] = after_ref[:, :tile_y, :]
    padded_ref[:, MARGIN - STEPS : MARGIN, :] = left_ref[:, :STEPS, :]
    padded_ref[:, MARGIN + tile_y : MARGIN + tile_y + STEPS, :] = right_ref[:, :STEPS, :]
    lane = lax.broadcasted_iota(jnp.int32, (high_x, members), 1)
    lines_ref[...] = jnp.zeros_like(lines_ref)
    for kind in range(kinds):
        base = kind * high_x
        lines_ref[base : base + STEPS, :] = before_ref[:, tile_y + kind, :]
        lines_ref[base + STEPS : base + STEPS + tile_x, :tile_y] = coefs_ref[kind]
        lines_ref[base + STEPS + tile_x : base + high_x, :] = after_ref[:, tile_y + kind, :]
        rows = slice(base, base + high_x)
        middle = pltpu.roll(lines_ref[rows, :], MARGIN, 1)
        left = pltpu.roll(left_ref[:, STEPS + kind, :], members + MARGIN - tile_y, 1)
        right = pltpu.roll(right_ref[:, STEPS + kind, :], MARGIN + tile_y, 1)
        line = jnp.where(lane < MARGIN, left, jnp.where(lane < MARGIN + tile_y, middle, right))
        near = (lane >= MARGIN - STEPS) & (lane < MARGIN + tile_y + STEPS)
        lines_ref[rows, :] = jnp.where(near, line, 0.0)
    columns_ref[...] = lines_ref[...].T
    width = 2 * STEPS + 1
    window = 24
    for slot in range(cells_ref.shape[0]):
        cell = cells_ref[slot]
        at_x = cell // tile_y
        at_y = cell % tile_y + (MARGIN - STEPS)
        start = pl.multiple_of(jnp.minimum(at_y // 8 * 8, high_y - window), 8)
        patch = [padded_ref[at_x + i, pl.ds(start, window), :] for i in range(width)]
        coefs = pltpu.roll(columns_ref[pl.ds(start, window), :], members - at_x, 1)
        for step in range(1, STEPS + 1):
            fresh = list(patch)
            for i in range(step, width - step):
                fresh[i] = advance(
                    patch[i - 1],
                    patch[i],
                    patch[i + 1],
                    *(coefs[:, k * high_x + i : k * high_x + i + 1] for k in range(kinds)),
                )
            patch = fresh
        last_ref[...] = patch[STEPS]
        prior = last_ref[pl.ds(at_y + STEPS - start, 1), :]
        for copy in range(copies):
            priors_ref[copy, slot : slot + 1, :] = prior


def look(copies, cells, field, coefs, before, after, left, right):
    tile_x, tile_y, members = field.shape
    high_x, high_y = tile_x + 2 * STEPS, tile_y + 2 * MARGIN
    return pl.pallas_call(
        functools.partial(look_kernel, copies),
        name="look",
        out_shape=(
            jax.ShapeDtypeStruct((high_x, high_y, members), jnp.float32),
            jax.ShapeDtypeStruct((members, members), jnp.float32),
            jax.ShapeDtypeStruct((copies, cells.shape[0], members), jnp.float32),
        ),
        in_specs=[in_smem()] + [in_vmem()] * 6,
        out_specs=(in_vmem(),) * 3,
        scratch_shapes=[
            pltpu.VMEM((members, members), jnp.float32),
            pltpu.VMEM((24, members), jnp.float32),
        ],
        compiler_params=grant(12),
    )(cells, field, coefs, before, after, left, right)


def forecast_kernel(kinds, padded_ref, columns_ref, out_ref, ping_ref, pong_ref, spread_ref):
    high_x, high_y, members = padded_ref.shape
    tile_y = high_y - 2 * MARGIN
    for index in range(kinds * high_x):
        spread_ref[index] = jnp.broadcast_to(
            columns_ref[:high_y, index : index + 1], (high_y, members)
        )
    source = padded_ref
    for step in range(1, STEPS + 1):
        final = step == STEPS
        target = (ping_ref, pong_ref)[step % 2]

        def one_row(x, carry):
            row = advance(
                source[x - 1],
                source[x],
                source[x + 1],
                *(spread_ref[kind * high_x + x] for kind in range(kinds)),
            )
            if final:
                where = pl.ds(pl.multiple_of((x - STEPS) * tile_y, tile_y), tile_y)
                out_ref[where, :] = row[MARGIN : MARGIN + tile_y]
            else:
                target[x] = row
            return carry

        lax.fori_loop(step, high_x - step, one_row, 0, unroll=2)
        source = target


def forecast(kinds, padded, columns):
    high_x, high_y, members = padded.shape
    tile_x, tile_y = high_x - 2 * STEPS, high_y - 2 * MARGIN
    work = STEPS * high_x * high_y * members
    return pl.pallas_call(
        functools.partial(forecast_kernel, kinds),
        name="forecast",
        out_shape=jax.ShapeDtypeStruct((tile_x * tile_y, members), jnp.float32),
        in_specs=[in_vmem()] * 2,
        out_specs=in_vmem(),
        scratch_shapes=[
            pltpu.VMEM((high_x, high_y, members), jnp.float32),
            pltpu.VMEM((high_x, high_y, members), jnp.float32),
            pltpu.VMEM((kinds * high_x, high_y, members), jnp.float32),
        ],
        compiler_params=grant(16),
        cost_estimate=pl.CostEstimate(
            flops=20 * work, bytes_accessed=8 * high_x * high_y * members, transcendentals=work
        ),
    )(padded, columns)


def share(rows, axis, count, groups=None):
    height, width = rows.shape
    copies = jnp.broadcast_to(rows[None], (count, height, width)).reshape(count * height, width)
    return lax.all_to_all(copies, axis, 0, 0, axis_index_groups=groups, tiled=True)


def along_planes(narrow, wide):
    ys, xs, cs = GY_FACTORS[narrow]

    def at(y, x, c):
        return (y * xs + x) * cs + c

    planes = [
        [z * narrow + at(y, x, c) for y in range(ys) for z in range(wide)]
        for x in range(xs)
        for c in range(cs)
    ]
    lines = [[at(y, x, c) for x in range(xs)] for y in range(ys) for c in range(cs)]
    across = [(i, i ^ 1) for i in range(narrow)]
    return planes, lines, across


def gather_kernel(rows_ref, rank_ref, first_ref, rest_ref):
    slots = rows_ref.shape[0]
    copies, room = first_ref.shape[0], first_ref.shape[1]
    rank = lax.broadcasted_iota(jnp.int32, (slots, slots), 0).astype(jnp.float32)
    pick = (rank == rank_ref[...]).astype(jnp.float32).astype(jnp.bfloat16)
    left = rows_ref[...]
    packed = jnp.zeros_like(left)
    for _ in range(3):
        part = left.astype(jnp.bfloat16)
        packed = packed + jnp.dot(pick, part, preferred_element_type=jnp.float32)
        left = left - part.astype(jnp.float32)
    for copy in range(copies):
        first_ref[copy] = packed[:room]
    rest_ref[...] = packed[room:]


def gather(rows, rank, copies, room):
    slots, members = rows.shape
    return pl.pallas_call(
        gather_kernel,
        name="gather",
        out_shape=(
            jax.ShapeDtypeStruct((copies, room, members), jnp.float32),
            jax.ShapeDtypeStruct((slots - room, members), jnp.float32),
        ),
        in_specs=[in_vmem()] * 2,
        out_specs=(in_vmem(),) * 2,
        compiler_params=grant(8),
    )(rows, rank)


def share_all(copies, rank, crowded, wide, narrow, beside):
    xs = GY_FACTORS[narrow][1]
    planes, lines, across = along_planes(narrow, wide)
    rows = lax.all_to_all(copies, ("gx", "gy"), 0, 0, axis_index_groups=planes, tiled=True)
    rows = rows.reshape(-1, rows.shape[-1])
    slots, members = rows.shape
    rows, rank, crowded, beside = lax.optimization_barrier((rows, rank, crowded, beside))
    first, rest = gather(rows, rank, xs, slots // 2)
    near = lax.all_to_all(first.reshape(-1, members), "gy", 0, 0, axis_index_groups=lines, tiled=True)
    far = lax.ppermute(near, "gy", across)

    def send(rest):
        near = share(rest, "gy", xs, lines)
        return near, lax.ppermute(near, "gy", across)

    def skip(rest):
        blank = jnp.zeros((xs * rest.shape[0], members), jnp.float32)
        return blank, blank

    more_near, more_far = lax.cond(crowded, send, skip, rest)
    return (near, far, more_near, more_far), beside


def local_cells(tile_id, obs_owner, obs_cell, obs_batch):
    span = 2048
    order = jnp.arange(obs_owner.shape[0], dtype=jnp.int32)
    key = (order * span + obs_cell)[None, :]
    batches = jnp.arange(BATCHES, dtype=jnp.int32)[:, None]
    mine = (obs_owner == tile_id)[None, :] & (obs_batch[None, :] == batches)
    first = jnp.min(jnp.where(mine, key, obs_owner.shape[0] * span), 1)
    last = jnp.max(jnp.where(mine, key, 0), 1)
    return jnp.stack([first, last], 1).reshape(-1) & (span - 1)


def locate(wide, narrow, owner):
    _, xs, cs = GY_FACTORS[narrow]
    row, col = owner // narrow, owner % narrow
    y, x, c = col // (xs * cs), col // cs % xs, col % cs
    return c * xs + x, y * wide + row


def sort(wide, narrow, owner, batch):
    count = owner.shape[0]
    ys, xs, cs = GY_FACTORS[narrow]
    plane, tile = locate(wide, narrow, owner)
    place = (batch * (xs * cs) + plane) * (ys * wide) + tile
    key = place * count + jnp.arange(count, dtype=jnp.int32)
    ahead = key[:, None] < key[None, :]
    position = jnp.sum(ahead.astype(jnp.int32), 0)
    second = jnp.sum((ahead & (place[:, None] == place[None, :])).astype(jnp.int32), 0)
    return position, second


def arrange(
    row_index, col_index, tile_x, tile_y, wide, narrow, owner, cell, batch, value, var, position, second
):
    count = owner.shape[0]
    ys, xs, cs = GY_FACTORS[narrow]
    number = xs * cs
    slots = ys * wide * BATCHES * CAP
    room = slots // 2
    side = col_index % cs
    own_plane = side * xs + col_index // cs % xs
    order = jnp.arange(count, dtype=jnp.int32)
    plane, tile = locate(wide, narrow, owner)
    group = batch * number + plane
    place = group * (ys * wide) + tile
    groups = jnp.arange(BATCHES * number, dtype=jnp.int32)
    member = (group[None, :] == groups[:, None]).astype(jnp.int32)
    held = jnp.sum(member, 1)
    before = jnp.sum(jnp.where(groups[None, :] < groups[:, None], held[None, :], 0), 1)
    base = jnp.concatenate([jnp.zeros((number,), jnp.int32), held[:number]])
    rank = position + jnp.sum(member * (base - before)[:, None], 0)
    crowded = jnp.any(held[:number] + held[number:] > room)
    slot = tile * (BATCHES * CAP) + batch * CAP + second
    here = (plane == own_plane)[None, :] & (
        slot[None, :] == jnp.arange(slots, dtype=jnp.int32)[:, None]
    )
    own_rank = (jnp.sum(jnp.where(here, rank[None, :] + 1, 0), 1) - 1).astype(jnp.float32)[None, :]
    shelf = ((plane // xs) ^ side) * xs + plane % xs
    source = jnp.where(
        rank < room,
        shelf * room + rank,
        number * room + shelf * (slots - room) + (rank - room),
    )
    px = owner // narrow * tile_x + cell // tile_y - row_index * tile_x
    py = owner % narrow * tile_y + cell % tile_y - col_index * tile_y
    pick = (position[None, :] == order[:, None]).astype(jnp.float32)
    table = jnp.stack(
        [
            source.astype(jnp.float32),
            place.astype(jnp.float32),
            px.astype(jnp.float32),
            py.astype(jnp.float32),
            value,
            var,
        ],
        0,
    )
    table = lax.dot_general(table, pick, (((1,), (1,)), ((), ())), precision=lax.Precision.HIGHEST)
    source = (table[0] + 0.5).astype(jnp.int32)
    place = table[1]
    edge = jnp.full((1,), -1.0, jnp.float32)
    follows = (place == jnp.concatenate([edge, place[:-1]])).astype(jnp.float32)
    leads = (place == jnp.concatenate([place[1:], edge])).astype(jnp.float32)

    def mate(row):
        zero = jnp.zeros((1,), jnp.float32)
        return leads * jnp.concatenate([row[1:], zero]) + follows * jnp.concatenate(
            [zero, row[:-1]]
        )

    rows = jnp.stack(
        [
            table[4],
            table[5],
            mate(table[4]),
            mate(table[5]) + (1.0 - leads - follows),
            leads,
            follows,
            table[2],
            table[3],
        ],
        0,
    )
    return source, rows, own_rank, crowded


def split(value):
    high = value.astype(jnp.bfloat16)
    low = (value - high.astype(jnp.float32)).astype(jnp.bfloat16)
    return high, low


def assimilate_kernel(
    tile_x,
    tile_y,
    reach_x,
    reach_y,
    source_ref,
    rows_ref,
    cols_ref,
    near_ref,
    far_ref,
    more_near_ref,
    more_far_ref,
    field_ref,
    out_ref,
    shared_ref,
    obs_ref,
    gain_a,
    gain_b,
    change_a,
    change_b,
    taper_x,
    taper_y,
):
    count, members = obs_ref.shape
    half = count // BATCHES
    scale_x = -0.5 / (reach_x * reach_x)
    scale_y = -0.5 / (reach_y * reach_y)

    start = 0
    for part_ref in (near_ref, far_ref, more_near_ref, more_far_ref):
        shared_ref[start : start + part_ref.shape[0], :] = part_ref[...]
        start += part_ref.shape[0]

    def fetch(index, carry):
        obs_ref[pl.ds(index, 1), :] = shared_ref[pl.ds(source_ref[index], 1), :]
        return carry

    lax.fori_loop(0, count, fetch, 0, unroll=8)

    def prepare(batch):
        low = batch * half
        prior = obs_ref[low : low + half, :]
        cols = cols_ref[low : low + half, :]
        value, var, mate_value, mate_var = (cols[:, i : i + 1] for i in range(4))
        leads, follows = cols[:, 4:5], cols[:, 5:6]
        mean = jnp.mean(prior, 1, keepdims=True)
        own = prior - mean
        after = pltpu.roll(prior, half - 1, 0)
        before = pltpu.roll(prior, 1, 0)
        mate_prior = jnp.where(leads > 0.0, after, before)
        mate_mean = jnp.mean(mate_prior, 1, keepdims=True)
        paired = leads + follows
        mate = (mate_prior - mate_mean) * paired
        own_own = jnp.sum(own * own, 1, keepdims=True)
        own_mate = jnp.sum(own * mate, 1, keepdims=True)
        rest = mate - own * (own_mate / jnp.maximum(own_own, 1e-30))
        area = own_own * jnp.sum(rest * rest, 1, keepdims=True)
        mate_mate = jnp.sum(mate * mate, 1, keepdims=True)
        floor = jnp.float32(members - 1)
        own_floor, mate_floor = floor * var, floor * mate_var
        det = own_floor * mate_floor + own_floor * mate_mate + mate_floor * own_own + area
        own_part = (mate_floor * own_own + area) / det
        mate_part = own_floor * own_mate / det
        shift = own_part * (value - mean) + mate_part * paired * (mate_value - mate_mean)
        change = shift - 0.5 * (own_part * own + mate_part * mate)
        gain = (own / (own_own + EPS)).T
        high, low_part = split(gain)
        gain_a[batch, :members, :] = high
        gain_a[batch, members:, :] = high
        gain_b[batch] = low_part
        high, low_part = split(change)
        change_a[batch, :, :members] = high
        change_a[batch, :, members:] = low_part
        change_b[batch] = high

    def increment(batch, cells, taper):
        anomaly = cells - jnp.mean(cells, 1, keepdims=True)
        high, low = split(anomaly)
        covary = jnp.dot(
            jnp.concatenate([high, low], 1), gain_a[batch], preferred_element_type=jnp.float32
        ) + jnp.dot(high, gain_b[batch], preferred_element_type=jnp.float32)
        high, low = split(covary * taper)
        both = jnp.dot(high, change_a[batch], preferred_element_type=jnp.float32)
        rest = jnp.dot(low, change_b[batch], preferred_element_type=jnp.float32)
        return cells + (both[:, :members] + both[:, members:] + rest)

    def update_field(batch, from_ref):
        low = batch * half
        obs_x = rows_ref[6:7, low : low + half]
        obs_y = rows_ref[7:8, low : low + half]
        at_x = lax.broadcasted_iota(jnp.int32, (tile_x, half), 0).astype(jnp.float32) - obs_x
        at_y = lax.broadcasted_iota(jnp.int32, (tile_y, half), 0).astype(jnp.float32) - obs_y
        taper_x[...] = jnp.exp(scale_x * (at_x * at_x))
        taper_y[...] = jnp.exp(scale_y * (at_y * at_y))

        for first in range(0, tile_x, GROUP):
            where = slice(first * tile_y, (first + GROUP) * tile_y)
            taper = jnp.concatenate(
                [taper_x[first + i : first + i + 1, :] * taper_y[...] for i in range(GROUP)], 0
            )
            out_ref[where, :] = increment(batch, from_ref[where, :], taper)

    prepare(0)
    chunk = min(half, 256)
    for start in range(half, count, chunk):
        gap_x = cols_ref[start : start + chunk, 6:7] - rows_ref[6:7, :half]
        gap_y = cols_ref[start : start + chunk, 7:8] - rows_ref[7:8, :half]
        taper = jnp.exp(scale_x * (gap_x * gap_x) + scale_y * (gap_y * gap_y))
        obs_ref[start : start + chunk, :] = increment(0, obs_ref[start : start + chunk, :], taper)
    prepare(1)
    update_field(0, field_ref)
    update_field(1, out_ref)


def assimilate(source, rows, cols, shared, field, tile_x, tile_y, reach_x, reach_y):
    cells, members = field.shape
    count = source.shape[0]
    half = count // BATCHES
    return pl.pallas_call(
        functools.partial(assimilate_kernel, tile_x, tile_y, reach_x, reach_y),
        name="assimilate",
        out_shape=jax.ShapeDtypeStruct((cells, members), jnp.float32),
        in_specs=[in_smem()] + [in_vmem()] * (3 + len(shared)),
        out_specs=in_vmem(),
        scratch_shapes=[
            pltpu.VMEM((sum(part.shape[0] for part in shared), members), jnp.float32),
            pltpu.VMEM((count, members), jnp.float32),
            pltpu.VMEM((BATCHES, 2 * members, half), jnp.bfloat16),
            pltpu.VMEM((BATCHES, members, half), jnp.bfloat16),
            pltpu.VMEM((BATCHES, half, 2 * members), jnp.bfloat16),
            pltpu.VMEM((BATCHES, half, members), jnp.bfloat16),
            pltpu.VMEM((tile_x, half), jnp.float32),
            pltpu.VMEM((tile_y, half), jnp.float32),
        ],
        compiler_params=grant(40),
    )(source, rows, cols, *shared, field)


def per_device(ensemble, coefficients, obs_owner, obs_cell, obs_batch, obs_value, obs_var):
    wide = lax.axis_size("gx")
    narrow = lax.axis_size("gy")
    row_index = lax.axis_index("gx")
    col_index = lax.axis_index("gy")
    tile_x, tile_y, members = ensemble.shape
    reach_x = tile_x * wide / 2.0
    reach_y = tile_y * narrow / 2.0
    cells = local_cells(row_index * narrow + col_index, obs_owner, obs_cell, obs_batch)
    position, second = sort(wide, narrow, obs_owner, obs_batch)
    first, last, coefs = pack_x(ensemble, coefficients)
    before, after = exchange(last, first, "gx")
    first, last = pack_y(ensemble, coefs, before, after)
    left, right = exchange(last, first, "gy")
    padded, columns, priors = look(
        wide * GY_FACTORS[narrow][0], cells, ensemble, coefs, before, after, left, right
    )
    priors, position, second = lax.optimization_barrier((priors, position, second))
    source, rows, rank, crowded = arrange(
        row_index,
        col_index,
        tile_x,
        tile_y,
        wide,
        narrow,
        obs_owner,
        obs_cell,
        obs_batch,
        obs_value,
        obs_var,
        position,
        second,
    )
    field = forecast(coefficients.shape[0], padded, columns)
    shared, (field, source, rows, cols) = share_all(
        priors, rank, crowded, wide, narrow, (field, source, rows, rows.T)
    )
    field = assimilate(
        source, rows, cols, shared, field, tile_x, tile_y, reach_x, reach_y
    )
    return field.reshape(tile_x, tile_y, members)


def solution(mesh):
    placed = (P("gx", "gy", None), P(None, "gx", "gy"), P(), P(), P(), P(), P())
    return jax.shard_map(
        per_device, mesh=mesh, in_specs=placed, out_specs=P("gx", "gy", None), check_vma=False
    )
```

profile of v0, /device:TPU:1, one launch (start us, length us, event | category | flops | bytes accessed | tf_op | source)
XLA Modules:
  0.0 98.2 jit_solution(17308942323347925400)
XLA Ops:
  0.0 0.0 copy-start
  0.0 1.1 %pack_x.1 = (f32[4,72,128]{2,1,0:T(8,128)S(1)}, f32[4,72,128]{2,1,0:T(8,128)S(1)}, f32[3,24,64]{2,1,0:T(8,128)S(1)}) custom-call(f32[24,64,128]{2,1,0:T(8,128)} %field_ref.5, f32[3,24,64]{2,1,0:T(8,128)} %whole_ref.1), custom_call_target="tpu_custom_call" | custom-call | tf_op jit(solution)/shard_map/pack_x/pallas_call | solution.py:72
  1.1 4.8 %collective-permute-start.1 = (f32[4,72,128]{2,1,0:T(8,128)S(1)}, f32[4,72,128]{2,1,0:T(8,128)S(1)}, u32[]{:S(2)}, u32[]{:S(2)}) collective-permute-start(f32[4,72,128]{2,1,0:T(8,128)S(1)} %get-tuple-element.29), channel_id=1, source_target_pairs={{0,64},{64,128},{128,192},{192,256},{256,320},{320,384},{384,448},... | collective-permute-start | bytes 442376 | tf_op jit(solution)/shard_map/ppermute | solution.py:26
  5.9 1.3 %collective-permute-start.2 = (f32[4,72,128]{2,1,0:T(8,128)S(1)}, f32[4,72,128]{2,1,0:T(8,128)S(1)}, u32[]{:S(2)}, u32[]{:S(2)}) collective-permute-start(f32[4,72,128]{2,1,0:T(8,128)S(1)} %get-tuple-element.30), channel_id=1, source_target_pairs={{64,0},{128,64},{192,128},{256,192},{320,256},{384,320},{448,384},... | collective-permute-start | bytes 442376 | tf_op jit(solution)/shard_map/ppermute | solution.py:26
  7.3 0.7 broadcast_compare_fusion.1
  8.0 0.7 fusion.25
  8.7 0.0 copy-start.1
  8.7 0.0 copy-start.2
  8.7 1.1 %convert_reduce_fusion = (s32[1024]{0:T(1024)S(1)}, s32[1024]{0:T(1024)S(1)}) fusion(s32[1024]{0:T(1024)S(1)} %get-tuple-element.79, s32[1024]{0:T(1024)S(1)} %iota_add_fusion), kind=kLoop, calls=%fused_computation.4 | loop fusion | flops 7337984 | bytes 16384 | tf_op jit(solution)/shard_map/reduce_sum | solution.py:370
  9.9 0.1 convert_reduce_fusion.1
  10.0 0.1 select_reduce_fusion.2
  10.1 0.0 copy-start.3
  10.2 0.0 copy-start.4
  10.2 0.1 pad_subtract_fusion
  10.3 0.8 compare_reduce_fusion
  11.0 0.8 select_reduce_fusion.4
  11.9 0.0 collective-permute-done.1.before_ref
  11.9 0.6 collective-permute-done.2.after_ref
  12.5 0.0 copy-done
  12.5 0.1 pack_y.1
  12.5 5.3 %collective-permute-start.3 = (f32[32,8,128]{2,1,0:T(8,128)S(1)}, f32[32,8,128]{2,1,0:T(8,128)S(1)}, u32[]{:S(2)}, u32[]{:S(2)}) collective-permute-start(f32[32,8,128]{2,1,0:T(8,128)S(1)} %get-tuple-element.31), channel_id=1, source_target_pairs={{0,1},{1,2},{2,3},{3,4},{4,5},{5,6},{6,7},{7,8},{8,9},{9,10},{10,1... | collective-permute-start | bytes 393224 | tf_op jit(solution)/shard_map/ppermute | solution.py:26
  17.8 5.4 %collective-permute-start.4 = (f32[32,8,128]{2,1,0:T(8,128)S(1)}, f32[32,8,128]{2,1,0:T(8,128)S(1)}, u32[]{:S(2)}, u32[]{:S(2)}) collective-permute-start(f32[32,8,128]{2,1,0:T(8,128)S(1)} %get-tuple-element.32), channel_id=1, source_target_pairs={{1,0},{2,1},{3,2},{4,3},{5,4},{6,5},{7,6},{8,7},{9,8},{10,9},{11,1... | collective-permute-start | bytes 393224 | tf_op jit(solution)/shard_map/ppermute | solution.py:26
  23.2 0.1 copy.21
  23.3 0.1 and.92.cells_ref
  23.4 0.1 select_reduce_fusion.1
  23.5 0.0 collective-permute-done.3.left_ref
  23.5 0.7 collective-permute-done.4.right_ref
  24.2 2.4 %look.1 = (f32[32,80,128]{2,1,0:T(8,128)S(1)}, f32[128,128]{1,0:T(8,128)S(1)}, f32[96,4,128]{2,1,0:T(4,128)}) custom-call(s32[4]{0:T(128)S(1)} %and.92.cells_ref, f32[24,64,128]{2,1,0:T(8,128)S(1)} %copy-done, f32[3,24,64]{2,1,0:T(8,128)S(1)} %get-tuple-element.28.coefs_ref, f32[4,72,128]{2,1,0:T(8,128)S(1)} %collective-permute-done.1.before_ref, ...), custom_call_target="tpu_custom_call" | custom-call | tf_op jit(solution)/shard_map/look/pallas_call | solution.py:198
  26.6 0.0 copy-done.1
  26.6 0.0 copy-done.2
  26.6 0.0 copy-done.3
  26.6 0.0 copy-done.4
  26.6 0.1 stack.47
  26.7 1.9 %fusion.1 = f32[6,1024]{1,0:T(8,128)S(1)} fusion(f32[6,1024]{1,0:T(8,128)S(1)} %stack.47, s32[1024]{0:T(1024)S(1)} %get-tuple-element.36), kind=kOutput, calls=%fused_computation.5 | convolution fusion | flops 76546048 | bytes 53248 | tf_op jit(solution)/shard_map/dot_general | solution.py:420
  28.6 0.1 fusion.42
  28.7 0.1 fusion.38
  28.8 0.1 subtract_add_fusion
  28.9 0.1 stack.48.rows_ref
  29.0 0.2 copy.22
  29.2 21.3 %all-to-all-start.1 = ((f32[96,4,128]{2,1,0:T(4,128)}), f32[96,4,128]{2,1,0:T(4,128)S(1)}, u32[]{:S(2)}, u32[]{:S(2)}) async-start(f32[96,4,128]{2,1,0:T(4,128)} %get-tuple-element.34), calls=%async_computation.1 | async-start | bytes 393216 | tf_op jit(solution)/shard_map/all_to_all | solution.py:324
  50.5 0.4 select_reduce_fusion
  50.9 4.8 %forecast.1.field_ref = f32[1536,128]{1,0:T(8,128)S(1)} custom-call(f32[32,80,128]{2,1,0:T(8,128)S(1)} %get-tuple-element.37.padded_ref, f32[128,128]{1,0:T(8,128)S(1)} %get-tuple-element.38.columns_ref), custom_call_target="tpu_custom_call" | custom-call | flops 26214400 | bytes 2621440 | tf_op jit(solution)/shard_map/forecast/pallas_call | solution.py:250
  55.7 9.0 %all-to-all-done.1 = f32[96,4,128]{2,1,0:T(4,128)S(1)} async-done(((f32[96,4,128]{2,1,0:T(4,128)}), f32[96,4,128]{2,1,0:T(4,128)S(1)}, u32[]{:S(2)}, u32[]{:S(2)}) %all-to-all-start.1) | async-done | bytes 196640 | tf_op jit(solution)/shard_map/all_to_all | solution.py:324
  64.7 0.4 gather.1
  65.1 14.2 %all_to_all.21 = f32[4,192,128]{2,1,0:T(8,128)S(1)} all-to-all(f32[4,192,128]{2,1,0:T(8,128)S(1)} %get-tuple-element.44), channel_id=1, replica_groups={{0,2,4,6},{1,3,5,7},{8,10,12,14},{9,11,13,15},{16,18,20,22},{17,19,21,2..., dimensions={0} | all-to-all | bytes 786432 | tf_op jit(solution)/shard_map/all_to_all | solution.py:329
  79.3 3.1 %collective-permute-start.5 = (f32[768,128]{1,0:T(8,128)S(1)}, f32[768,128]{1,0:T(8,128)S(1)}, u32[]{:S(2)}, u32[]{:S(2)}) collective-permute-start(f32[768,128]{1,0:T(8,128)S(1)} %bitcast.17), channel_id=1, source_target_pairs={{0,1},{1,0},{2,3},{3,2},{4,5},{5,4},{6,7},{7,6},{8,9},{9,8},{10,11... | collective-permute-start | bytes 1179656 | tf_op jit(solution)/shard_map/ppermute | solution.py:330
  83.1 1.6 %conditional.1 = (f32[768,128]{1,0:T(8,128)}, f32[768,128]{1,0:T(8,128)}) conditional(s32[]{:T(128)} %convert_element_type.67, () %tuple.17, f32[192,128]{1,0:T(8,128)S(1)} %get-tuple-element.46), branch_computations={%region_9.10_spmd, %region_10.11_spmd} | conditional | bytes 2850872 | solution.py:340
  83.1 0.8 broadcast.112
  83.9 0.8 broadcast.112.clone
  84.6 0.0 collective-permute-done.5.far_ref
  84.6 13.5 %assimilate.1 = f32[1536,128]{1,0:T(8,128)} custom-call(s32[1024]{0:T(1024)S(1)} %bitcast.20, f32[8,1024]{1,0:T(8,128)S(1)} %stack.48.rows_ref, f32[1024,8]{1,0:T(8,128)S(1)} %bitcast.16, f32[768,128]{1,0:T(8,128)S(1)} %bitcast.18, f32[768,128]{1,0:T(8,128)S(1)} %collective-permute-done.5.far_ref, f32[768,128]{1,0:T(8,128)} %get-tuple-element.47.more_near_ref, ...), custom_call_target="tpu_custom_call" | custom-call | tf_op jit(solution)/shard_map/assimilate/pallas_call | solution.py:573
  (8 shorter events, 0.1 us)
Async XLA Ops:
  0.0 12.5 %copy-start = (f32[24,64,128]{2,1,0:T(8,128)S(1)}, f32[24,64,128]{2,1,0:T(8,128)}, u32[]{:S(2)}) copy-start(f32[24,64,128]{2,1,0:T(8,128)} %field_ref.5) | copy-start | bytes 2359300
  1.1 10.8 %collective-permute-start.1 = (f32[4,72,128]{2,1,0:T(8,128)S(1)}, f32[4,72,128]{2,1,0:T(8,128)S(1)}, u32[]{:S(2)}, u32[]{:S(2)}) collective-permute-start(f32[4,72,128]{2,1,0:T(8,128)S(1)} %get-tuple-element.29), channel_id=1, source_target_pairs={{0,64},{64,128},{128,192},{192,256},{256,320},{320,384},{384,448},... | collective-permute-start | bytes 442376 | tf_op jit(solution)/shard_map/ppermute | solution.py:26
  5.9 6.5 %collective-permute-start.2 = (f32[4,72,128]{2,1,0:T(8,128)S(1)}, f32[4,72,128]{2,1,0:T(8,128)S(1)}, u32[]{:S(2)}, u32[]{:S(2)}) collective-permute-start(f32[4,72,128]{2,1,0:T(8,128)S(1)} %get-tuple-element.30), channel_id=1, source_target_pairs={{64,0},{128,64},{192,128},{256,192},{320,256},{384,320},{448,384},... | collective-permute-start | bytes 442376 | tf_op jit(solution)/shard_map/ppermute | solution.py:26
  8.7 17.9 %copy-start.1 = (s32[1024]{0:T(1024)S(1)}, s32[1024]{0:T(1024)}, u32[]{:S(2)}) copy-start(s32[1024]{0:T(1024)} %param.11) | copy-start | bytes 12292
  8.7 17.9 %copy-start.2 = (s32[1024]{0:T(1024)S(1)}, s32[1024]{0:T(1024)}, u32[]{:S(2)}) copy-start(s32[1024]{0:T(1024)} %param.13) | copy-start | bytes 12292
  10.1 16.5 %copy-start.3 = (f32[1024]{0:T(1024)S(1)}, f32[1024]{0:T(1024)}, u32[]{:S(2)}) copy-start(f32[1024]{0:T(1024)} %param.14) | copy-start | bytes 12292
  10.2 16.5 %copy-start.4 = (f32[1024]{0:T(1024)S(1)}, f32[1024]{0:T(1024)}, u32[]{:S(2)}) copy-start(f32[1024]{0:T(1024)} %param.15) | copy-start | bytes 12292
  12.5 11.0 %collective-permute-start.3 = (f32[32,8,128]{2,1,0:T(8,128)S(1)}, f32[32,8,128]{2,1,0:T(8,128)S(1)}, u32[]{:S(2)}, u32[]{:S(2)}) collective-permute-start(f32[32,8,128]{2,1,0:T(8,128)S(1)} %get-tuple-element.31), channel_id=1, source_target_pairs={{0,1},{1,2},{2,3},{3,4},{4,5},{5,6},{6,7},{7,8},{8,9},{9,10},{10,1... | collective-permute-start | bytes 393224 | tf_op jit(solution)/shard_map/ppermute | solution.py:26
  17.8 6.4 %collective-permute-start.4 = (f32[32,8,128]{2,1,0:T(8,128)S(1)}, f32[32,8,128]{2,1,0:T(8,128)S(1)}, u32[]{:S(2)}, u32[]{:S(2)}) collective-permute-start(f32[32,8,128]{2,1,0:T(8,128)S(1)} %get-tuple-element.32), channel_id=1, source_target_pairs={{1,0},{2,1},{3,2},{4,3},{5,4},{6,5},{7,6},{8,7},{9,8},{10,9},{11,1... | collective-permute-start | bytes 393224 | tf_op jit(solution)/shard_map/ppermute | solution.py:26
  29.2 35.5 %all-to-all-start.1 = ((f32[96,4,128]{2,1,0:T(4,128)}), f32[96,4,128]{2,1,0:T(4,128)S(1)}, u32[]{:S(2)}, u32[]{:S(2)}) async-start(f32[96,4,128]{2,1,0:T(4,128)} %get-tuple-element.34), calls=%async_computation.1 | async-start | bytes 393216 | tf_op jit(solution)/shard_map/all_to_all | solution.py:324
  79.3 5.4 %collective-permute-start.5 = (f32[768,128]{1,0:T(8,128)S(1)}, f32[768,128]{1,0:T(8,128)S(1)}, u32[]{:S(2)}, u32[]{:S(2)}) collective-permute-start(f32[768,128]{1,0:T(8,128)S(1)} %bitcast.17), channel_id=1, source_target_pairs={{0,1},{1,0},{2,3},{3,2},{4,5},{5,4},{6,7},{7,6},{8,9},{9,8},{10,11... | collective-permute-start | bytes 1179656 | tf_op jit(solution)/shard_map/ppermute | solution.py:330
where the time goes:
time: 98.6 us; the launch traced here: 98.2 us
  starting transfers between devices  41.2 us (42%)
  Pallas kernels  22.3 us (23%)
  blocking collectives  14.2 us (14%)
  waiting for transfers between devices  10.2 us (10%)
  other arithmetic  5.25 us (5%)
  local copies, waits for them, and re-layouts  2.16 us (2%)
  matrix products  1.92 us (2%)
    all_to_all x1, starting transfers between devices, share_all(): lax.all_to_all(copies, ('gx', 'gy'), 0, 0, axis_index_groups=planes, tile...  21.3 us
    all_to_all x1, blocking collectives, share_all(): lax.all_to_all(first.reshape(-1, members), 'gy', 0, 0, axis_index_groups=...  14.2 us
    pallas_call x1, Pallas kernels, assimilate(): pl.pallas_call(functools.partial(assimilate_kernel, tile_x, tile_y, reach...  13.5 us
    ppermute x2, starting transfers between devices, exchange(): lax.ppermute(to_next, axis, up)  10.1 us
    all_to_all x1, waiting for transfers between devices, share_all(): lax.all_to_all(copies, ('gx', 'gy'), 0, 0, axis_index_groups=planes, tile...  8.97 us
    ppermute x2, starting transfers between devices, exchange(): lax.ppermute(to_previous, axis, down)  6.69 us
    pallas_call x1, Pallas kernels, forecast(): pl.pallas_call(functools.partial(forecast_kernel, kinds), name='forecast'...  4.78 us
    ppermute x1, starting transfers between devices, share_all(): far = lax.ppermute(near, 'gy', across)  3.12 us
  transfers between devices with their start and end apart: 6, of which 3 were waited for; matrix products, arithmetic and copies ran while one was open for 7% of the time, Pallas kernels for 5%

commit v1 on v0

--- a/solution.py
+++ b/solution.py
@@ -136,6 +136,7 @@
     priors_ref,
     lines_ref,
     last_ref,
+    found_ref,
 ):
     tile_x, tile_y, members = field_ref.shape
     kinds = coefs_ref.shape[0]
@@ -186,10 +187,11 @@
                     *(coefs[:, k * high_x + i : k * high_x + i + 1] for k in range(kinds)),
                 )
             patch = fresh
-        last_ref[...] = patch[STEPS]
-        prior = last_ref[pl.ds(at_y + STEPS - start, 1), :]
-        for copy in range(copies):
-            priors_ref[copy, slot : slot + 1, :] = prior
+        last_ref[slot] = patch[STEPS]
+        found_ref[slot : slot + 1, :] = last_ref[slot, pl.ds(at_y + STEPS - start, 1), :]
+    found = found_ref[: cells_ref.shape[0], :]
+    for copy in range(copies):
+        priors_ref[copy] = found
 
 
 def look(copies, cells, field, coefs, before, after, left, right):
@@ -207,7 +209,8 @@
         out_specs=(in_vmem(),) * 3,
         scratch_shapes=[
             pltpu.VMEM((members, members), jnp.float32),
-            pltpu.VMEM((24, members), jnp.float32),
+            pltpu.VMEM((cells.shape[0], 24, members), jnp.float32),
+            pltpu.VMEM((8, members), jnp.float32),
         ],
         compiler_params=grant(12),
     )(cells, field, coefs, before, after, left, right)
@@ -318,6 +321,14 @@
     )(rows, rank)
 
 
+def unread(shape):
+    array = jax.ShapeDtypeStruct(shape, jnp.float32)
+    anywhere = pl.BlockSpec(memory_space=pl.ANY)
+    return pl.pallas_call(
+        lambda *refs: None, name="unread", out_shape=(array, array), out_specs=(anywhere, anywhere)
+    )()
+
+
 def share_all(copies, rank, crowded, wide, narrow, beside):
     xs = GY_FACTORS[narrow][1]
     planes, lines, across = along_planes(narrow, wide)
@@ -334,8 +345,7 @@
         return near, lax.ppermute(near, "gy", across)
 
     def skip(rest):
-        blank = jnp.zeros((xs * rest.shape[0], members), jnp.float32)
-        return blank, blank
+        return unread((xs * rest.shape[0], members))
 
     more_near, more_far = lax.cond(crowded, send, skip, rest)
     return (near, far, more_near, more_far), beside
@@ -419,6 +429,7 @@
     )
     table = lax.dot_general(table, pick, (((1,), (1,)), ((), ())), precision=lax.Precision.HIGHEST)
     source = (table[0] + 0.5).astype(jnp.int32)
+    source = jnp.concatenate([source, jnp.broadcast_to(crowded.astype(jnp.int32), (8,))])
     place = table[1]
     edge = jnp.full((1,), -1.0, jnp.float32)
     follows = (place == jnp.concatenate([edge, place[:-1]])).astype(jnp.float32)
@@ -474,16 +485,29 @@
     change_b,
     taper_x,
     taper_y,
+    sems,
 ):
     count, members = obs_ref.shape
     half = count // BATCHES
     scale_x = -0.5 / (reach_x * reach_x)
     scale_y = -0.5 / (reach_y * reach_y)
 
-    start = 0
-    for part_ref in (near_ref, far_ref, more_near_ref, more_far_ref):
-        shared_ref[start : start + part_ref.shape[0], :] = part_ref[...]
-        start += part_ref.shape[0]
+    first, more = near_ref.shape[0], more_near_ref.shape[0]
+    shared_ref[:first, :] = near_ref[...]
+    shared_ref[first : 2 * first, :] = far_ref[...]
+
+    @pl.when(source_ref[count] > 0)
+    def _():
+        copies = [
+            pltpu.make_async_copy(
+                part_ref, shared_ref.at[pl.ds(2 * first + i * more, more)], sems.at[i]
+            )
+            for i, part_ref in enumerate((more_near_ref, more_far_ref))
+        ]
+        for copy in copies:
+            copy.start()
+        for copy in copies:
+            copy.wait()
 
     def fetch(index, carry):
         obs_ref[pl.ds(index, 1), :] = shared_ref[pl.ds(source_ref[index], 1), :]
@@ -568,13 +592,18 @@
 
 def assimilate(source, rows, cols, shared, field, tile_x, tile_y, reach_x, reach_y):
     cells, members = field.shape
-    count = source.shape[0]
+    count = rows.shape[1]
     half = count // BATCHES
+    near, far, *more = shared
+    more = [pltpu.with_memory_space_constraint(part, pltpu.HBM) for part in more]
     return pl.pallas_call(
         functools.partial(assimilate_kernel, tile_x, tile_y, reach_x, reach_y),
         name="assimilate",
         out_shape=jax.ShapeDtypeStruct((cells, members), jnp.float32),
-        in_specs=[in_smem()] + [in_vmem()] * (3 + len(shared)),
+        in_specs=[in_smem()]
+        + [in_vmem()] * 4
+        + [pl.BlockSpec(memory_space=pl.ANY)] * 2
+        + [in_vmem()],
         out_specs=in_vmem(),
         scratch_shapes=[
             pltpu.VMEM((sum(part.shape[0] for part in shared), members), jnp.float32),
@@ -585,9 +614,10 @@
             pltpu.VMEM((BATCHES, half, members), jnp.bfloat16),
             pltpu.VMEM((tile_x, half), jnp.float32),
             pltpu.VMEM((tile_y, half), jnp.float32),
+            pltpu.SemaphoreType.DMA((2,)),
         ],
         compiler_params=grant(40),
-    )(source, rows, cols, *shared, field)
+    )(source, rows, cols, near, far, *more, field)
 
 
 def per_device(ensemble, coefficients, obs_owner, obs_cell, obs_batch, obs_value, obs_var):

time: 98.6 us -> 97.3 us (0.987)
  local copies, waits for them, and re-layouts: 2.16 us -> 0.63 us
    another operation x2 -> x0, local copies, waits for them, and re-layouts: 1.54 us -> none
  transfers between devices with their start and end apart: 6 -> 6, of which waited for: 3 -> 4; matrix products, arithmetic and copies ran while one was open for 7% -> 5% of each run, Pallas kernels for 5% -> 5%
where the time goes in v1:
time: 97.3 us; the launch traced here: 96.8 us
  starting transfers between devices  41.2 us (42%)
  Pallas kernels  21.7 us (22%)
  blocking collectives  14.2 us (15%)
  waiting for transfers between devices  10.2 us (10%)
  other arithmetic  5.16 us (5%)
  matrix products  1.92 us (2%)
  between operations  1.55 us (2%)
    all_to_all x1, starting transfers between devices, share_all(): lax.all_to_all(copies, ('gx', 'gy'), 0, 0, axis_index_groups=planes, tile...  21.3 us
    all_to_all x1, blocking collectives, share_all(): lax.all_to_all(first.reshape(-1, members), 'gy', 0, 0, axis_index_groups=...  14.2 us
    pallas_call x1, Pallas kernels, assimilate(): pl.pallas_call(functools.partial(assimilate_kernel, tile_x, tile_y, reach...  13 us
    ppermute x2, starting transfers between devices, exchange(): lax.ppermute(to_next, axis, up)  10.1 us
    all_to_all x1, waiting for transfers between devices, share_all(): lax.all_to_all(copies, ('gx', 'gy'), 0, 0, axis_index_groups=planes, tile...  8.92 us
    ppermute x2, starting transfers between devices, exchange(): lax.ppermute(to_previous, axis, down)  6.69 us
    pallas_call x1, Pallas kernels, forecast(): pl.pallas_call(functools.partial(forecast_kernel, kinds), name='forecast'...  4.81 us
    ppermute x1, starting transfers between devices, share_all(): far = lax.ppermute(near, 'gy', across)  3.13 us
  transfers between devices with their start and end apart: 6, of which 4 were waited for; matrix products, arithmetic and copies ran while one was open for 5% of the time, Pallas kernels for 5%

profile of v1, /device:TPU:1, one launch (start us, length us, event | category | flops | bytes accessed | tf_op | source)
XLA Modules:
  0.0 96.8 jit_solution(16761518957579629388)
XLA Ops:
  0.0 0.0 copy-start
  0.0 1.1 %pack_x.1 = (f32[4,72,128]{2,1,0:T(8,128)S(1)}, f32[4,72,128]{2,1,0:T(8,128)S(1)}, f32[3,24,64]{2,1,0:T(8,128)S(1)}) custom-call(f32[24,64,128]{2,1,0:T(8,128)} %field_ref.5, f32[3,24,64]{2,1,0:T(8,128)} %whole_ref.1), custom_call_target="tpu_custom_call" | custom-call | tf_op jit(solution)/shard_map/pack_x/pallas_call | solution.py:72
  1.1 4.8 %collective-permute-start.1 = (f32[4,72,128]{2,1,0:T(8,128)S(1)}, f32[4,72,128]{2,1,0:T(8,128)S(1)}, u32[]{:S(2)}, u32[]{:S(2)}) collective-permute-start(f32[4,72,128]{2,1,0:T(8,128)S(1)} %get-tuple-element.29), channel_id=1, source_target_pairs={{0,64},{64,128},{128,192},{192,256},{256,320},{320,384},{384,448},... | collective-permute-start | bytes 442376 | tf_op jit(solution)/shard_map/ppermute | solution.py:26
  5.9 1.3 %collective-permute-start.2 = (f32[4,72,128]{2,1,0:T(8,128)S(1)}, f32[4,72,128]{2,1,0:T(8,128)S(1)}, u32[]{:S(2)}, u32[]{:S(2)}) collective-permute-start(f32[4,72,128]{2,1,0:T(8,128)S(1)} %get-tuple-element.30), channel_id=1, source_target_pairs={{64,0},{128,64},{192,128},{256,192},{320,256},{384,320},{448,384},... | collective-permute-start | bytes 442376 | tf_op jit(solution)/shard_map/ppermute | solution.py:26
  7.3 0.7 broadcast_compare_fusion.1
  8.0 0.7 fusion.25
  8.7 0.0 copy-start.1
  8.7 0.0 copy-start.2
  8.7 1.1 %convert_reduce_fusion = (s32[1024]{0:T(1024)S(1)}, s32[1024]{0:T(1024)S(1)}) fusion(s32[1024]{0:T(1024)S(1)} %get-tuple-element.79, s32[1024]{0:T(1024)S(1)} %iota_add_fusion), kind=kLoop, calls=%fused_computation.4 | loop fusion | flops 7337984 | bytes 16384 | tf_op jit(solution)/shard_map/reduce_sum | solution.py:380
  9.9 0.1 convert_reduce_fusion.1
  10.0 0.1 select_reduce_fusion.2
  10.1 0.0 copy-start.3
  10.2 0.0 copy-start.4
  10.2 0.1 pad_subtract_fusion
  10.3 0.7 compare_reduce_fusion
  10.9 0.8 select_reduce_fusion.4
  11.8 0.0 collective-permute-done.1.before_ref
  11.8 0.6 collective-permute-done.2.after_ref
  12.5 0.0 copy-done
  12.5 0.1 pack_y.1
  12.5 5.3 %collective-permute-start.3 = (f32[32,8,128]{2,1,0:T(8,128)S(1)}, f32[32,8,128]{2,1,0:T(8,128)S(1)}, u32[]{:S(2)}, u32[]{:S(2)}) collective-permute-start(f32[32,8,128]{2,1,0:T(8,128)S(1)} %get-tuple-element.31), channel_id=1, source_target_pairs={{0,1},{1,2},{2,3},{3,4},{4,5},{5,6},{6,7},{7,8},{8,9},{9,10},{10,1... | collective-permute-start | bytes 393224 | tf_op jit(solution)/shard_map/ppermute | solution.py:26
  17.8 5.4 %collective-permute-start.4 = (f32[32,8,128]{2,1,0:T(8,128)S(1)}, f32[32,8,128]{2,1,0:T(8,128)S(1)}, u32[]{:S(2)}, u32[]{:S(2)}) collective-permute-start(f32[32,8,128]{2,1,0:T(8,128)S(1)} %get-tuple-element.32), channel_id=1, source_target_pairs={{1,0},{2,1},{3,2},{4,3},{5,4},{6,5},{7,6},{8,7},{9,8},{10,9},{11,1... | collective-permute-start | bytes 393224 | tf_op jit(solution)/shard_map/ppermute | solution.py:26
  23.2 0.1 copy.21
  23.3 0.1 and.92.cells_ref
  24.0 0.1 select_reduce_fusion.1
  24.1 0.0 collective-permute-done.3.left_ref
  24.1 0.1 collective-permute-done.4.right_ref
  24.2 2.4 %look.1 = (f32[32,80,128]{2,1,0:T(8,128)S(1)}, f32[128,128]{1,0:T(8,128)S(1)}, f32[96,4,128]{2,1,0:T(4,128)}) custom-call(s32[4]{0:T(128)S(1)} %and.92.cells_ref, f32[24,64,128]{2,1,0:T(8,128)S(1)} %copy-done, f32[3,24,64]{2,1,0:T(8,128)S(1)} %get-tuple-element.28.coefs_ref, f32[4,72,128]{2,1,0:T(8,128)S(1)} %collective-permute-done.1.before_ref, ...), custom_call_target="tpu_custom_call" | custom-call | tf_op jit(solution)/shard_map/look/pallas_call | solution.py:200
  26.6 0.0 copy-done.1
  26.6 0.0 copy-done.2
  26.6 0.0 copy-done.3
  26.6 0.0 copy-done.4
  26.6 0.1 stack.47
  26.7 1.9 %fusion.1 = f32[6,1024]{1,0:T(8,128)S(1)} fusion(f32[6,1024]{1,0:T(8,128)S(1)} %stack.47, s32[1024]{0:T(1024)S(1)} %get-tuple-element.36), kind=kOutput, calls=%fused_computation.5 | convolution fusion | flops 76546048 | bytes 53248 | tf_op jit(solution)/shard_map/dot_general | solution.py:430
  28.6 0.1 fusion.42
  28.7 0.1 fusion.38
  28.8 0.1 subtract_add_fusion
  28.9 0.1 stack.48.rows_ref
  29.0 0.2 copy.22
  29.2 21.3 %all-to-all-start.1 = ((f32[96,4,128]{2,1,0:T(4,128)}), f32[96,4,128]{2,1,0:T(4,128)S(1)}, u32[]{:S(2)}, u32[]{:S(2)}) async-start(f32[96,4,128]{2,1,0:T(4,128)} %get-tuple-element.34), calls=%async_computation.1 | async-start | bytes 393216 | tf_op jit(solution)/shard_map/all_to_all | solution.py:335
  50.5 0.4 select_reduce_fusion
  50.9 4.8 %forecast.1.field_ref = f32[1536,128]{1,0:T(8,128)S(1)} custom-call(f32[32,80,128]{2,1,0:T(8,128)S(1)} %get-tuple-element.37.padded_ref, f32[128,128]{1,0:T(8,128)S(1)} %get-tuple-element.38.columns_ref), custom_call_target="tpu_custom_call" | custom-call | flops 26214400 | bytes 2621440 | tf_op jit(solution)/shard_map/forecast/pallas_call | solution.py:253
  55.7 8.9 %all-to-all-done.1 = f32[96,4,128]{2,1,0:T(4,128)S(1)} async-done(((f32[96,4,128]{2,1,0:T(4,128)}), f32[96,4,128]{2,1,0:T(4,128)S(1)}, u32[]{:S(2)}, u32[]{:S(2)}) %all-to-all-start.1) | async-done | bytes 196640 | tf_op jit(solution)/shard_map/all_to_all | solution.py:335
  64.7 0.4 gather.1
  65.1 14.2 %all_to_all.21 = f32[4,192,128]{2,1,0:T(8,128)S(1)} all-to-all(f32[4,192,128]{2,1,0:T(8,128)S(1)} %get-tuple-element.44), channel_id=1, replica_groups={{0,2,4,6},{1,3,5,7},{8,10,12,14},{9,11,13,15},{16,18,20,22},{17,19,21,2..., dimensions={0} | all-to-all | bytes 786432 | tf_op jit(solution)/shard_map/all_to_all | solution.py:340
  79.2 3.1 %collective-permute-start.5 = (f32[768,128]{1,0:T(8,128)S(1)}, f32[768,128]{1,0:T(8,128)S(1)}, u32[]{:S(2)}, u32[]{:S(2)}) collective-permute-start(f32[768,128]{1,0:T(8,128)S(1)} %bitcast.17), channel_id=1, source_target_pairs={{0,1},{1,0},{2,3},{3,2},{4,5},{5,4},{6,7},{7,6},{8,9},{9,8},{10,11... | collective-permute-start | bytes 1179656 | tf_op jit(solution)/shard_map/ppermute | solution.py:341
  82.9 0.2 conditional.1
  83.1 0.6 collective-permute-done.5.far_ref
  83.7 13.0 %assimilate.1 = f32[1536,128]{1,0:T(8,128)} custom-call(s32[1032]{0:T(1024)S(1)} %concatenate.35.source_ref, f32[8,1024]{1,0:T(8,128)S(1)} %stack.48.rows_ref, f32[1024,8]{1,0:T(8,128)S(1)} %bitcast.16, f32[768,128]{1,0:T(8,128)S(1)} %bitcast.18, f32[768,128]{1,0:T(8,128)S(1)} %collective-permute-done.5.far_ref, f32[768,128]{1,0:T(8,128)} %get-tuple-element.47.more_near_ref, ...), custom_call_target="tpu_custom_call" | custom-call | tf_op jit(solution)/shard_map/assimilate/pallas_call | solution.py:599
  (10 shorter events, 0.1 us)
Async XLA Ops:
  0.0 12.5 %copy-start = (f32[24,64,128]{2,1,0:T(8,128)S(1)}, f32[24,64,128]{2,1,0:T(8,128)}, u32[]{:S(2)}) copy-start(f32[24,64,128]{2,1,0:T(8,128)} %field_ref.5) | copy-start | bytes 2359300
  1.1 10.7 %collective-permute-start.1 = (f32[4,72,128]{2,1,0:T(8,128)S(1)}, f32[4,72,128]{2,1,0:T(8,128)S(1)}, u32[]{:S(2)}, u32[]{:S(2)}) collective-permute-start(f32[4,72,128]{2,1,0:T(8,128)S(1)} %get-tuple-element.29), channel_id=1, source_target_pairs={{0,64},{64,128},{128,192},{192,256},{256,320},{320,384},{384,448},... | collective-permute-start | bytes 442376 | tf_op jit(solution)/shard_map/ppermute | solution.py:26
  5.9 6.5 %collective-permute-start.2 = (f32[4,72,128]{2,1,0:T(8,128)S(1)}, f32[4,72,128]{2,1,0:T(8,128)S(1)}, u32[]{:S(2)}, u32[]{:S(2)}) collective-permute-start(f32[4,72,128]{2,1,0:T(8,128)S(1)} %get-tuple-element.30), channel_id=1, source_target_pairs={{64,0},{128,64},{192,128},{256,192},{320,256},{384,320},{448,384},... | collective-permute-start | bytes 442376 | tf_op jit(solution)/shard_map/ppermute | solution.py:26
  8.7 17.9 %copy-start.1 = (s32[1024]{0:T(1024)S(1)}, s32[1024]{0:T(1024)}, u32[]{:S(2)}) copy-start(s32[1024]{0:T(1024)} %param.11) | copy-start | bytes 12292
  8.7 17.8 %copy-start.2 = (s32[1024]{0:T(1024)S(1)}, s32[1024]{0:T(1024)}, u32[]{:S(2)}) copy-start(s32[1024]{0:T(1024)} %param.13) | copy-start | bytes 12292
  10.1 16.5 %copy-start.3 = (f32[1024]{0:T(1024)S(1)}, f32[1024]{0:T(1024)}, u32[]{:S(2)}) copy-start(f32[1024]{0:T(1024)} %param.14) | copy-start | bytes 12292
  10.2 16.4 %copy-start.4 = (f32[1024]{0:T(1024)S(1)}, f32[1024]{0:T(1024)}, u32[]{:S(2)}) copy-start(f32[1024]{0:T(1024)} %param.15) | copy-start | bytes 12292
  12.5 11.5 %collective-permute-start.3 = (f32[32,8,128]{2,1,0:T(8,128)S(1)}, f32[32,8,128]{2,1,0:T(8,128)S(1)}, u32[]{:S(2)}, u32[]{:S(2)}) collective-permute-start(f32[32,8,128]{2,1,0:T(8,128)S(1)} %get-tuple-element.31), channel_id=1, source_target_pairs={{0,1},{1,2},{2,3},{3,4},{4,5},{5,6},{6,7},{7,8},{8,9},{9,10},{10,1... | collective-permute-start | bytes 393224 | tf_op jit(solution)/shard_map/ppermute | solution.py:26
  17.8 6.4 %collective-permute-start.4 = (f32[32,8,128]{2,1,0:T(8,128)S(1)}, f32[32,8,128]{2,1,0:T(8,128)S(1)}, u32[]{:S(2)}, u32[]{:S(2)}) collective-permute-start(f32[32,8,128]{2,1,0:T(8,128)S(1)} %get-tuple-element.32), channel_id=1, source_target_pairs={{1,0},{2,1},{3,2},{4,3},{5,4},{6,5},{7,6},{8,7},{9,8},{10,9},{11,1... | collective-permute-start | bytes 393224 | tf_op jit(solution)/shard_map/ppermute | solution.py:26
  29.2 35.5 %all-to-all-start.1 = ((f32[96,4,128]{2,1,0:T(4,128)}), f32[96,4,128]{2,1,0:T(4,128)S(1)}, u32[]{:S(2)}, u32[]{:S(2)}) async-start(f32[96,4,128]{2,1,0:T(4,128)} %get-tuple-element.34), calls=%async_computation.1 | async-start | bytes 393216 | tf_op jit(solution)/shard_map/all_to_all | solution.py:335
  79.2 4.5 %collective-permute-start.5 = (f32[768,128]{1,0:T(8,128)S(1)}, f32[768,128]{1,0:T(8,128)S(1)}, u32[]{:S(2)}, u32[]{:S(2)}) collective-permute-start(f32[768,128]{1,0:T(8,128)S(1)} %bitcast.17), channel_id=1, source_target_pairs={{0,1},{1,0},{2,3},{3,2},{4,5},{5,4},{6,7},{7,6},{8,9},{9,8},{10,11... | collective-permute-start | bytes 1179656 | tf_op jit(solution)/shard_map/ppermute | solution.py:341
